TPU v7x, 128 devices: a whole 4x4x4 slice. The times are simulated.
128 devices in a mesh: path: 16 (over x_hi, y, core), shard: 8 (over x_lo, z).
Axes of the slice: x: 4 (x_hi: 2, x_lo: 2; x = x_hi * 2 + x_lo), y: 4, z: 4, core: 2. Of those that a mesh axis runs over, the one named last changes fastest.
Arguments:
- path_params: bfloat16 [16, 16, 64, 4096], P('path', None, 'shard'), may hold values from -6 to 6
- global_params: float32 [256, 64, 4096], P('path', 'shard'), may hold values from -6 to 6
- momentum: float32 [256, 64, 4096], P('path', 'shard'), may hold values from -6 to 6
- module_ids: int32 [16, 16], replicated, may hold values from 0 to 255, as said below
- token_counts: int32 [16, 16], replicated, may hold values from 16 to 256
Outputs:
- new_global: float32 [256, 64, 4096], P('path', 'shard')
- new_momentum: float32 [256, 64, 4096], P('path', 'shard')
- path_modules: bfloat16 [16, 16, 64, 4096], P('path', None, 'shard')
Inputs may be any that keep to these rules, and one draw needn't show every extreme that they name: `module_ids`: each row names 16 different modules. Among the modules of one row, at most 2 lie in any one block of 16 consecutive module numbers, and every row has exactly 2 in some block.
All inputs are finite; a program needn't handle non-finite values.
Results may differ from a plain program's by a relative error of at most 0.0004.
Values may be sent and summed in bfloat16 or wider, within the bound.
A program may use at most 128 MiB of HBM per device.

v0:
```python
import jax
import jax.numpy as jnp
from jax import lax
from jax.sharding import PartitionSpec as P

CAP = 2


outer_momentum = 0.9
outer_rate = 0.7


def from_everyone(x, axis):
    copies = jnp.broadcast_to(x, (lax.axis_size(axis), *x.shape))
    return lax.all_to_all(copies, axis, split_axis=0, concat_axis=0, tiled=True)


def of_everyone(x, axis):
    return from_everyone(x, axis).sum(axis=0)


def on_device(path_params, global_params, momentum, module_ids, token_counts):
    paths, held = module_ids.shape
    owned = global_params.shape[0]
    rows = path_params.shape[2]
    width = path_params.shape[3]
    span = rows * width
    owner = lax.axis_index("path")
    local = path_params.reshape(held, span)
    counts = token_counts.astype(jnp.float32)
    targets = owner * owned + jnp.arange(owned, dtype=jnp.int32)
    match = module_ids[None, :, :] == targets[:, None, None]
    total = jnp.sum(jnp.where(match, counts[None, :, :], 0.0), axis=(1, 2))
    groups = module_ids // owned
    places = jnp.arange(held, dtype=jnp.int32)
    before = (groups[:, None, :] == groups[:, :, None]) & (places[None, :] < places[:, None])[
        None, :, :
    ]
    earlier = jnp.sum(before.astype(jnp.int32), axis=2)
    my_group = lax.dynamic_index_in_dim(groups, owner, 0, keepdims=False)
    my_earlier = lax.dynamic_index_in_dim(earlier, owner, 0, keepdims=False)
    slot_owner = jnp.arange(paths * CAP, dtype=jnp.int32) // CAP
    slot_rank = jnp.arange(paths * CAP, dtype=jnp.int32) % CAP
    ranks = jnp.arange(CAP, dtype=jnp.int32)
    slot_match = match[:, :, None, :] & (earlier[None, :, None, :] == ranks[None, None, :, None])
    select = (
        (my_group[None, :] == slot_owner[:, None]) & (my_earlier[None, :] == slot_rank[:, None])
    ).astype(jnp.bfloat16)
    outgoing = (
        jnp.dot(select, local, preferred_element_type=jnp.float32)
        .astype(jnp.bfloat16)
        .reshape(paths, CAP, span)
    )
    incoming = lax.all_to_all(outgoing, "path", split_axis=0, concat_axis=0, tiled=True)
    weights = jnp.sum(jnp.where(slot_match, counts[None, :, None, :], 0.0), axis=3)
    summed = jnp.dot(
        weights.reshape(owned, paths * CAP).astype(jnp.bfloat16),
        incoming.reshape(paths * CAP, span),
        preferred_element_type=jnp.float32,
    )
    params = global_params.reshape(owned, span)
    past = momentum.reshape(owned, span)
    raw = (total[:, None] * params - summed) / jnp.maximum(total, 1.0)[:, None]
    squares = of_everyone(jnp.sum(raw * raw, axis=1), "shard")
    mean_square = squares / (span * lax.axis_size("shard"))
    factor = jnp.minimum(1.0, 1.0 / jnp.sqrt(mean_square + 1e-06))
    delta = raw * factor[:, None]
    velocity = outer_momentum * past + delta
    updated = params - outer_rate * (outer_momentum * velocity + delta)
    rounded = updated.astype(jnp.bfloat16)
    back_select = jnp.any(slot_match, axis=3).astype(jnp.bfloat16)
    back_select = jnp.transpose(back_select, (1, 2, 0)).reshape(paths * CAP, owned)
    outgoing_back = (
        jnp.dot(back_select, rounded, preferred_element_type=jnp.float32)
        .astype(jnp.bfloat16)
        .reshape(paths, CAP, span)
    )
    arriving = lax.all_to_all(outgoing_back, "path", split_axis=0, concat_axis=0, tiled=True)
    place = (
        (my_group[:, None] == slot_owner[None, :]) & (my_earlier[:, None] == slot_rank[None, :])
    ).astype(jnp.bfloat16)
    received = jnp.dot(
        place, arriving.reshape(paths * CAP, span), preferred_element_type=jnp.float32
    )
    path_out = received.astype(jnp.bfloat16).reshape(1, held, rows, width)
    return (updated.reshape(global_params.shape), velocity.reshape(momentum.shape), path_out)


def solution(mesh):
    placed = (
        P("path", None, "shard", None),
        P("path", "shard", None),
        P("path", "shard", None),
        P(),
        P(),
    )
    return jax.shard_map(
        on_device,
        mesh=mesh,
        in_specs=placed,
        out_specs=(
            P("path", "shard", None),
            P("path", "shard", None),
            P("path", None, "shard", None),
        ),
        check_vma=False,
    )
```

profile of v0, /device:TPU:1, one launch (start us, length us, event | category | flops | bytes accessed | tf_op | source)
XLA Modules:
  0.0 112.3 jit_solution(10023566114668034767)
XLA Ops:
  0.7 0.7 add_select_fusion
  1.4 1.8 %copy.20 = bf16[2,8,8,4096]{3,1,2,0:T(8,128)(2,1)S(1)} copy(bf16[2,8,8,4096]{3,2,1,0:T(8,128)(2,1)} %bitcast.40) | data formatting | bytes 2097152
  3.2 0.4 convert_reduce_fusion
  3.6 0.7 convolution_convert_fusion.1
  4.4 2.6 %reshape.133 = bf16[16,2,32768]{2,1,0:T(2,128)(2,1)} reshape(bf16[32,32768]{1,0:T(8,128)(2,1)S(1)} %convolution_convert_fusion.1) | data formatting | bytes 4194304 | tf_op jit(solution)/shard_map/reshape | solution.py:52
  7.0 8.6 %all-to-all-start = ((bf16[16,2,32768]{2,1,0:T(2,128)(2,1)}), bf16[16,2,32768]{2,1,0:T(2,128)(2,1)}, u32[]{:S(2)}, u32[]{:S(2)}) async-start(bf16[16,2,32768]{2,1,0:T(2,128)(2,1)} %reshape.133), calls=%async_computation | async-start | bytes 4194304 | tf_op jit(solution)/shard_map/all_to_all | solution.py:54
  15.6 2.5 %copy.18 = f32[2,8,8,4096]{3,1,2,0:T(8,128)} copy(f32[2,8,8,4096]{3,2,1,0:T(8,128)S(1)} %bitcast.37) | data formatting | bytes 4194304
  19.0 25.0 %all-to-all-done = bf16[16,2,32768]{2,1,0:T(2,128)(2,1)} async-done(((bf16[16,2,32768]{2,1,0:T(2,128)(2,1)}), bf16[16,2,32768]{2,1,0:T(2,128)(2,1)}, u32[]{:S(2)}, u32[]{:S(2)}) %all-to-all-start) | async-done | bytes 2097184 | tf_op jit(solution)/shard_map/all_to_all | solution.py:54
  44.0 5.0 %multiply_reduce_fusion = (f32[16]{0:T(128)S(1)}, f32[16,32768]{1,0:T(8,128)}) fusion(f32[16]{0:T(128)S(1)} %broadcast_maximum_fusion, bf16[16,2,32768]{2,1,0:T(2,128)(2,1)} %all-to-all-done, bf16[16,16,2]{1,2,0:T(2,128)(2,1)S(1)} %fusion.4, f32[16,32768]{1,0:T(8,128)} %bitcast.31, f32[16]{0:T(128)S(1)} %select_reduce_fusion), kind=kOutput, calls=%fused_computation.8 | convolution fusion | flops 36175856 | bytes 6292672 | tf_op jit(solution)/shard_map/dot_general | solution.py:56
  49.0 0.6 broadcast_in_dim.26
  49.6 5.6 %all-to-all-start.1 = ((f32[8,1,16]{2,1,0:T(1,128)}), f32[8,1,16]{2,1,0:T(1,128)S(1)}, u32[]{:S(2)}, u32[]{:S(2)}) async-start(f32[8,1,16]{2,1,0:T(1,128)} %broadcast_in_dim.26), calls=%async_computation.1 | async-start | bytes 8192 | tf_op jit(solution)/shard_map/all_to_all | solution.py:15
  55.2 0.6 and_reduce_fusion
  55.9 2.5 %copy.19 = f32[2,8,8,4096]{3,1,2,0:T(8,128)} copy(f32[2,8,8,4096]{3,2,1,0:T(8,128)S(1)} %bitcast.30) | data formatting | bytes 4194304
  58.5 1.6 %all-to-all-done.1 = f32[8,1,16]{2,1,0:T(1,128)S(1)} async-done(((f32[8,1,16]{2,1,0:T(1,128)}), f32[8,1,16]{2,1,0:T(1,128)S(1)}, u32[]{:S(2)}, u32[]{:S(2)}) %all-to-all-start.1) | async-done | bytes 544 | tf_op jit(solution)/shard_map/all_to_all | solution.py:15
  60.1 4.7 %multiply_add_fusion = (f32[16,32768]{1,0:T(8,128)}, f32[16,32768]{1,0:T(8,128)S(1)}) fusion(f32[16,32768]{1,0:T(8,128)} %bitcast.33, f32[16,32768]{1,0:T(8,128)} %get-tuple-element.6, f32[16]{0:T(128)S(1)} %rsqrt_minimum_fusion, f32[16,32768]{1,0:T(8,128)} %bitcast.32), kind=kLoop, calls=%fused_computation.9 | loop fusion | flops 3145728 | bytes 10485824 | tf_op jit(solution)/shard_map/add | solution.py:68
  64.8 2.0 %convolution_convert_fusion = bf16[32,32768]{1,0:T(8,128)(2,1)} fusion(pred[32,16]{1,0:T(32,128)(4,1)S(1)} %reshape.136, f32[16,32768]{1,0:T(8,128)S(1)} %get-tuple-element.4), kind=kOutput, calls=%fused_computation | convolution fusion | flops 35127296 | bytes 4194816 | tf_op jit(solution)/shard_map/dot_general | solution.py:74
  66.8 4.4 %reshape.137 = bf16[16,2,32768]{2,1,0:T(2,128)(2,1)} reshape(bf16[32,32768]{1,0:T(8,128)(2,1)} %convolution_convert_fusion) | data formatting | bytes 4194304 | tf_op jit(solution)/shard_map/reshape | solution.py:76
  71.2 7.8 %all-to-all-start.2 = ((bf16[16,2,32768]{2,1,0:T(2,128)(2,1)}), bf16[16,2,32768]{2,1,0:T(2,128)(2,1)}, u32[]{:S(2)}, u32[]{:S(2)}) async-start(bf16[16,2,32768]{2,1,0:T(2,128)(2,1)} %reshape.137), calls=%async_computation.2 | async-start | bytes 4194304 | tf_op jit(solution)/shard_map/all_to_all | solution.py:78
  79.0 4.1 %copy.22 = f32[2,8,8,4096]{3,2,1,0:T(8,128)} copy(f32[2,8,8,4096]{3,1,2,0:T(8,128)} %bitcast.34) | data formatting | bytes 4194304
  83.2 2.5 %copy.21 = f32[2,8,8,4096]{3,2,1,0:T(8,128)} copy(f32[2,8,8,4096]{3,1,2,0:T(8,128)S(1)} %bitcast.29) | data formatting | bytes 4194304
  85.7 21.8 %all-to-all-done.2 = bf16[16,2,32768]{2,1,0:T(2,128)(2,1)} async-done(((bf16[16,2,32768]{2,1,0:T(2,128)(2,1)}), bf16[16,2,32768]{2,1,0:T(2,128)(2,1)}, u32[]{:S(2)}, u32[]{:S(2)}) %all-to-all-start.2) | async-done | bytes 2097184 | tf_op jit(solution)/shard_map/all_to_all | solution.py:78
  107.5 2.8 %reshape.138 = bf16[32,32768]{1,0:T(8,128)(2,1)S(1)} reshape(bf16[16,2,32768]{2,1,0:T(2,128)(2,1)} %all-to-all-done.2) | data formatting | bytes 4194304 | tf_op jit(solution)/shard_map/reshape | solution.py:83
  110.3 0.5 convolution_convert_fusion.2
  110.8 1.5 %copy.23 = bf16[2,8,8,4096]{3,2,1,0:T(8,128)(2,1)} copy(bf16[2,8,8,4096]{3,1,2,0:T(8,128)(2,1)S(1)} %bitcast.36) | data formatting | bytes 2097152
  (23 shorter events, 1.0 us)
Async XLA Ops:
  7.0 8.6 %copy-start.3 = (s32[16,16]{1,0:T(8,128)S(1)}, s32[16,16]{1,0:T(8,128)}, u32[]{:S(2)}) copy-start(s32[16,16]{1,0:T(8,128)} %param.9) | copy-start | bytes 3076
  7.0 8.6 %copy-start = (f32[16,8,4096]{2,1,0:T(8,128)S(1)}, f32[16,8,4096]{2,1,0:T(8,128)}, u32[]{:S(2)}) copy-start(f32[16,8,4096]{2,1,0:T(8,128)} %param.6) | copy-start | bytes 6291460
  7.0 37.0 %all-to-all-start = ((bf16[16,2,32768]{2,1,0:T(2,128)(2,1)}), bf16[16,2,32768]{2,1,0:T(2,128)(2,1)}, u32[]{:S(2)}, u32[]{:S(2)}) async-start(bf16[16,2,32768]{2,1,0:T(2,128)(2,1)} %reshape.133), calls=%async_computation | async-start | bytes 4194304 | tf_op jit(solution)/shard_map/all_to_all | solution.py:54
  15.6 2.6 %copy-start.2 = (s32[16,16]{1,0:T(8,128)S(1)}, s32[16,16]{1,0:T(8,128)}, u32[]{:S(2)}) copy-start(s32[16,16]{1,0:T(8,128)} %param.8) | copy-start | bytes 3076
  15.6 3.1 %copy-start.1 = (f32[16,8,4096]{2,1,0:T(8,128)S(1)}, f32[16,8,4096]{2,1,0:T(8,128)}, u32[]{:S(2)}) copy-start(f32[16,8,4096]{2,1,0:T(8,128)} %param.7) | copy-start | bytes 6291460
  49.6 10.5 %all-to-all-start.1 = ((f32[8,1,16]{2,1,0:T(1,128)}), f32[8,1,16]{2,1,0:T(1,128)S(1)}, u32[]{:S(2)}, u32[]{:S(2)}) async-start(f32[8,1,16]{2,1,0:T(1,128)} %broadcast_in_dim.26), calls=%async_computation.1 | async-start | bytes 8192 | tf_op jit(solution)/shard_map/all_to_all | solution.py:15
  71.2 36.3 %all-to-all-start.2 = ((bf16[16,2,32768]{2,1,0:T(2,128)(2,1)}), bf16[16,2,32768]{2,1,0:T(2,128)(2,1)}, u32[]{:S(2)}, u32[]{:S(2)}) async-start(bf16[16,2,32768]{2,1,0:T(2,128)(2,1)} %reshape.137), calls=%async_computation.2 | async-start | bytes 4194304 | tf_op jit(solution)/shard_map/all_to_all | solution.py:78
where the time goes:
time: 113 us; the launch traced here: 112 us
  waiting for transfers between devices  48.4 us (43%)
  local copies, waits for them, and re-layouts  25.6 us (23%)
  starting transfers between devices  22 us (19%)
  matrix products  8.22 us (7%)
  other arithmetic  7.26 us (6%)
    all_to_all x1, waiting for transfers between devices, on_device(): lax.all_to_all(outgoing, 'path', split_axis=0, concat_axis=0, tiled=True)  25 us
    all_to_all x1, waiting for transfers between devices, on_device(): lax.all_to_all(outgoing_back, 'path', split_axis=0, concat_axis=0, tiled=...  21.8 us
    unnamed x14, local copies, waits for them, and re-layouts  15.1 us
    all_to_all x1, starting transfers between devices, on_device(): lax.all_to_all(outgoing, 'path', split_axis=0, concat_axis=0, tiled=True)  8.56 us
    all_to_all x1, starting transfers between devices, on_device(): lax.all_to_all(outgoing_back, 'path', split_axis=0, concat_axis=0, tiled=...  7.84 us
    all_to_all x1, starting transfers between devices, from_everyone(): return lax.all_to_all(copies, axis, split_axis=0, concat_axis=0, tiled=True)  5.56 us
    dot_general x1, matrix products, on_device(): jnp.dot(weights.reshape(owned, paths * CAP).astype(jnp.bfloat16), incomin...  4.98 us
    add x1, other arithmetic, on_device(): velocity = outer_momentum * past + delta  4.66 us
  transfers between devices with their start and end apart: 3, of which 3 were waited for; matrix products, arithmetic and copies ran while one was open for 12% of the time, Pallas kernels for 0%

commit v1 on v0

v1 whole, which is shorter than its diff:
```python
import functools

import jax
import jax.numpy as jnp
from jax import lax
from jax.experimental import pallas as pl
from jax.experimental.pallas import tpu as pltpu
from jax.sharding import PartitionSpec as P

MESH = pl.DeviceIdType.MESH
CAP = 2
CHUNKS = 4
LANES = 128

outer_momentum = 0.9
outer_rate = 0.7

ORDER = (
    (0, 1, 0), (0, 3, 0), (1, 0, 0), (0, 2, 0), (1, 1, 0), (1, 3, 0), (1, 2, 0),
    (0, 1, 1), (0, 3, 1), (1, 0, 1), (0, 2, 1), (1, 1, 1), (1, 3, 1), (1, 2, 1),
    (0, 0, 1),
)


def number(offset):
    return (offset[0] * 4 + offset[1]) * 2 + offset[2]


def path_at(me, offset, sign):
    x, y, c = me // 8, (me // 2) % 4, me % 2
    x = (x + offset[0]) % 2
    y = (y + sign * offset[1] + 4) % 4
    c = (c + offset[2]) % 2
    return (x * 4 + y) * 2 + c


def offset_of(index):
    return (index // 8, (index // 2) % 4, index % 2)


def kernel(
    ids_ref, counts_ref, params_ref, global_ref, momentum_ref,
    new_global_ref, new_momentum_ref, placed_ref,
    *scratch, paths, owned, held, shards, rows, chunks, span,
):
    (ids, counts, local, glob, mom, out, raw, squares, mine, others, factor,
     rounded, out_back, new_glob, new_mom, placed, pick_v, table_v, weight_v,
     pick, table, weight) = scratch[:22]
    arrived = scratch[22:22 + chunks]
    back = scratch[22 + chunks:22 + 2 * chunks]
    (load_sem, send_sem, recv_sem, back_sem, norm_send, norm_recv, store_sem) = scratch[22 + 2 * chunks:]
    me = lax.axis_index("path")
    shard = lax.axis_index("shard")
    block = rows // chunks

    load_ids = pltpu.make_async_copy(ids_ref, ids, load_sem.at[0])
    load_counts = pltpu.make_async_copy(counts_ref, counts, load_sem.at[1])
    load_local = pltpu.make_async_copy(params_ref, local, load_sem.at[2])
    load_glob = pltpu.make_async_copy(global_ref, glob, load_sem.at[3])
    load_mom = pltpu.make_async_copy(momentum_ref, mom, load_sem.at[4])
    for load in (load_ids, load_counts, load_local, load_glob, load_mom):
        load.start()
    barrier = pltpu.get_barrier_semaphore()
    for offset in ORDER:
        pl.semaphore_signal(
            barrier, inc=1, device_id=(path_at(me, offset, 1), shard), device_id_type=MESH
        )
    zl = shards // 2
    shard_offsets = [(a, b) for a in range(2) for b in range(zl)][1:]

    def shard_at(a, b):
        return ((shard // zl + a) % 2) * zl + (shard % zl + b) % zl

    for a, b in shard_offsets:
        pl.semaphore_signal(barrier, inc=1, device_id=(me, shard_at(a, b)), device_id_type=MESH)

    lane = lax.broadcasted_iota(jnp.int32, (paths, LANES), 1)
    sub = lax.broadcasted_iota(jnp.int32, (paths, LANES), 0)
    place = lax.broadcasted_iota(jnp.int32, (paths, held), 1)
    load_ids.wait()
    load_counts.wait()
    all_ids = ids[...]
    group = lax.shift_right_logical(all_ids, 4)
    my_group = lax.shift_right_logical(ids[pl.ds(me, 1), :], 4)
    rowid = lax.broadcasted_iota(jnp.int32, (paths, held), 0)
    goes = my_group == rowid
    first = jnp.min(jnp.where(goes, place, held - 1), axis=1, keepdims=True)
    last = jnp.max(jnp.where(goes, place, 0), axis=1, keepdims=True)
    pick_v[...] = jnp.where(lane == 0, first, last)
    copy_pick = pltpu.make_async_copy(pick_v, pick, load_sem.at[0])
    copy_pick.start()

    ours = group == me
    local_ids = all_ids - me * owned
    from_first = jnp.min(jnp.where(ours, place, held - 1), axis=1, keepdims=True)
    from_last = jnp.max(jnp.where(ours, place, 0), axis=1, keepdims=True)
    first_id = jnp.sum(jnp.where(ours & (place == from_first), local_ids, 0), axis=1, keepdims=True)
    last_id = jnp.sum(jnp.where(ours & (place == from_last), local_ids, 0), axis=1, keepdims=True)
    tab = jnp.where(lane == owned, first_id, last_id)
    amount = jnp.zeros((paths, LANES), jnp.float32)
    tokens = counts[...].astype(jnp.float32)
    for m in range(owned):
        same = local_ids == m
        spot = jnp.sum(jnp.where(same, place, 0), axis=1, keepdims=True)
        slot = jnp.where(spot == from_first, 0, 1)
        tab = jnp.where(lane == m, slot, tab)
        amount = jnp.where(
            lane == m, jnp.sum(jnp.where(same, tokens, 0.0), axis=1, keepdims=True), amount
        )
    rank = jnp.sum(jnp.where(goes & (place != first), 1, 0), axis=0, keepdims=True)
    gx = lax.shift_right_logical(my_group, 3)
    gy = lax.shift_right_logical(my_group, 1) & 3
    gc = my_group & 1
    ox = (gx + me // 8) & 1
    oy = ((me // 2) % 4 + 4 - gy) & 3
    oc = (gc + me % 2) & 1
    where_from = ((ox * 4 + oy) * 2 + oc) * CAP + rank
    table_v[0:paths, :] = tab
    table_v[paths:paths + 1, 0:held] = where_from
    sums = jnp.sum(amount, axis=0, keepdims=True)
    weight_v[0:paths, :] = amount
    weight_v[paths:paths + 1, :] = sums
    weight_v[paths + 1:paths + 2, :] = 1.0 / jnp.maximum(sums, 1.0)
    copy_table = pltpu.make_async_copy(table_v, table, load_sem.at[1])
    copy_weight = pltpu.make_async_copy(weight_v, weight, load_sem.at[5])
    copy_table.start()
    copy_weight.start()

    load_local.wait()
    copy_pick.wait()
    for index in (0, *map(number, ORDER)):
        goal = path_at(me, offset_of(index), 1)
        for r in range(CAP):
            k = pick[goal, r]
            for c in range(chunks):
                piece = local[k, c * block:(c + 1) * block, :]
                if index == 0:
                    arrived[c][0, r] = piece
                else:
                    out[c, index, r] = piece
    pl.semaphore_wait(barrier, len(ORDER) + len(shard_offsets))

    def send(source, target, recv, c, offset, sign):
        index = number(offset)
        return pltpu.make_async_remote_copy(
            src_ref=source.at[c, index],
            dst_ref=target[c].at[index],
            send_sem=send_sem.at[c, index],
            recv_sem=recv.at[c, index],
            device_id=(path_at(me, offset, sign), shard),
            device_id_type=MESH,
        )

    for c in range(chunks):
        for offset in ORDER:
            send(out, arrived, recv_sem, c, offset, 1).start()

    copy_table.wait()
    copy_weight.wait()
    load_glob.wait()
    load_mom.wait()
    for c in range(chunks):
        for offset in ORDER:
            send(out, arrived, recv_sem, c, offset, 1).wait_recv()

        def one_sum(m, carry, c=c):
            acc = jnp.zeros((block, LANES), jnp.float32)
            for index in range(paths):
                source = path_at(me, offset_of(index), -1)
                x = arrived[c][index, table[source, m]]
                acc = acc + weight[source, m] * x.astype(jnp.float32)
            part = (weight[paths, m] * glob[m, c * block:(c + 1) * block, :] - acc) * weight[paths + 1, m]
            raw[c, m] = part
            squared = jnp.sum((part * part).reshape(block // 8, 8, LANES), axis=0)
            if c == 0:
                squares[m] = squared
            else:
                squares[m] += squared
            return carry

        lax.fori_loop(0, owned, one_sum, 0)

    mine[...] = jnp.sum(squares[...], axis=1)
    norms = []
    for j, (a, b) in enumerate(shard_offsets):
        norm = pltpu.make_async_remote_copy(
            src_ref=mine,
            dst_ref=others.at[j],
            send_sem=norm_send.at[j],
            recv_sem=norm_recv.at[j],
            device_id=(me, shard_at(a, b)),
            device_id_type=MESH,
        )
        norm.start()
        norms.append(norm)
    for c in range(chunks):
        for offset in ORDER:
            send(out, arrived, recv_sem, c, offset, 1).wait_send()
    for norm in norms:
        norm.wait()
    whole = mine[...]
    for j in range(len(shard_offsets)):
        whole = whole + others[j]
    mean = jnp.sum(whole, axis=1, keepdims=True) / span
    factor[...] = jnp.broadcast_to(
        jnp.minimum(1.0, 1.0 / jnp.sqrt(mean + 1e-06)), (owned, LANES)
    )

    stores = []
    for c in range(chunks):
        here = slice(c * block, (c + 1) * block)

        def update(m, carry, c=c, here=here):
            delta = raw[c, m] * factor[pl.ds(m, 1), :]
            velocity = outer_momentum * mom[m, here, :] + delta
            updated = glob[m, here, :] - outer_rate * (outer_momentum * velocity + delta)
            new_mom[c, m] = velocity
            new_glob[c, m] = updated
            rounded[m] = updated.astype(jnp.bfloat16)
            return carry

        lax.fori_loop(0, owned, update, 0)
        for index in (0, *map(number, ORDER)):
            goal = path_at(me, offset_of(index), 1)
            for r in range(CAP):
                piece = rounded[table[goal, owned + r]]
                if index == 0:
                    back[c][r] = piece
                else:
                    out_back[c, index, r] = piece
        for offset in ORDER:
            index = number(offset)
            pltpu.make_async_remote_copy(
                src_ref=out_back.at[c, index],
                dst_ref=back[c].at[pl.ds(index * CAP, CAP)],
                send_sem=send_sem.at[c, index],
                recv_sem=back_sem.at[c, index],
                device_id=(path_at(me, offset, 1), shard),
                device_id_type=MESH,
            ).start()
        for j, (source, target) in enumerate(((new_glob, new_global_ref), (new_mom, new_momentum_ref))):
            store = pltpu.make_async_copy(
                source.at[c], target.at[:, pl.ds(c * block, block), :], store_sem.at[j, c]
            )
            store.start()
            stores.append(store)

    for c in range(chunks):
        for offset in ORDER:
            index = number(offset)
            pltpu.make_async_remote_copy(
                src_ref=out_back.at[c, index],
                dst_ref=back[c].at[pl.ds(index * CAP, CAP)],
                send_sem=send_sem.at[c, index],
                recv_sem=back_sem.at[c, index],
                device_id=(path_at(me, offset, 1), shard),
                device_id_type=MESH,
            ).wait_recv()
        for k in range(held):
            placed[c, k] = back[c][table[paths, k]]
        store = pltpu.make_async_copy(
            placed.at[c], placed_ref.at[:, pl.ds(c * block, block), :], store_sem.at[2, c]
        )
        store.start()
        stores.append(store)
    for c in range(chunks):
        for offset in ORDER:
            index = number(offset)
            pltpu.make_async_remote_copy(
                src_ref=out_back.at[c, index],
                dst_ref=back[c].at[pl.ds(index * CAP, CAP)],
                send_sem=send_sem.at[c, index],
                recv_sem=back_sem.at[c, index],
                device_id=(path_at(me, offset, 1), shard),
                device_id_type=MESH,
            ).wait_send()
    for store in stores:
        store.wait()


def to_tiles(x):
    n, r, w = x.shape
    return x.reshape(n, r, w // LANES, LANES).transpose(0, 2, 1, 3).reshape(n, r * w // LANES, LANES)


def from_tiles(x, r):
    n, rows, _ = x.shape
    w = rows * LANES // r
    return x.reshape(n, w // LANES, r, LANES).transpose(0, 2, 1, 3).reshape(n, r, w)


def on_device(path_params, global_params, momentum, module_ids, token_counts):
    paths, held = module_ids.shape
    owned, r, width = global_params.shape
    shards = lax.axis_size("shard")
    rows = r * width // LANES
    chunks = CHUNKS
    block = rows // chunks
    bf, f32, i32 = jnp.bfloat16, jnp.float32, jnp.int32
    vmem, smem = pltpu.VMEM, pltpu.SMEM
    dma = pltpu.SemaphoreType.DMA
    hbm = pl.BlockSpec(memory_space=pl.ANY)
    scratch = [
        vmem((paths, held), i32), vmem((paths, held), i32),
        vmem((held, rows, LANES), bf), vmem((owned, rows, LANES), f32), vmem((owned, rows, LANES), f32),
        vmem((chunks, paths, CAP, block, LANES), bf),
        vmem((chunks, owned, block, LANES), f32),
        vmem((owned, 8, LANES), f32), vmem((owned, LANES), f32), vmem((shards - 1, owned, LANES), f32),
        vmem((owned, LANES), f32),
        vmem((owned, block, LANES), bf),
        vmem((chunks, paths, CAP, block, LANES), bf),
        vmem((chunks, owned, block, LANES), f32), vmem((chunks, owned, block, LANES), f32),
        vmem((chunks, held, block, LANES), bf),
        vmem((paths, LANES), i32), vmem((paths + 8, LANES), i32), vmem((paths + 8, LANES), f32),
        smem((paths, LANES), i32), smem((paths + 8, LANES), i32), smem((paths + 8, LANES), f32),
        *[vmem((paths, CAP, block, LANES), bf) for _ in range(chunks)],
        *[vmem((paths * CAP, block, LANES), bf) for _ in range(chunks)],
        dma((6,)), dma((chunks, paths)), dma((chunks, paths)), dma((chunks, paths)),
        dma((shards - 1,)), dma((shards - 1,)), dma((3, chunks)),
    ]
    new_global, new_momentum, placed = pl.pallas_call(
        functools.partial(
            kernel, paths=paths, owned=owned, held=held, shards=shards, rows=rows,
            chunks=chunks, span=r * width * shards,
        ),
        out_shape=(
            jax.ShapeDtypeStruct((owned, rows, LANES), f32),
            jax.ShapeDtypeStruct((owned, rows, LANES), f32),
            jax.ShapeDtypeStruct((held, rows, LANES), bf),
        ),
        in_specs=[hbm] * 5,
        out_specs=(hbm, hbm, hbm),
        scratch_shapes=scratch,
        compiler_params=pltpu.CompilerParams(
            collective_id=0, has_side_effects=True, vmem_limit_bytes=48 * 1024 * 1024
        ),
    )(module_ids, token_counts, to_tiles(path_params[0]), to_tiles(global_params), to_tiles(momentum))
    return (
        from_tiles(new_global, r),
        from_tiles(new_momentum, r),
        from_tiles(placed, r)[None],
    )


def solution(mesh):
    placed = (
        P("path", None, "shard", None),
        P("path", "shard", None),
        P("path", "shard", None),
        P(),
        P(),
    )
    return jax.shard_map(
        on_device,
        mesh=mesh,
        in_specs=placed,
        out_specs=(
            P("path", "shard", None),
            P("path", "shard", None),
            P("path", None, "shard", None),
        ),
        check_vma=False,
    )
```

time: 113 us -> 77 us (0.68)
  Pallas kernels: 0 us -> 68.9 us
  waiting for transfers between devices: 48.4 us -> 0 us
  starting transfers between devices: 22 us -> 0 us
  local copies, waits for them, and re-layouts: 25.6 us -> 7.24 us
  matrix products: 8.22 us -> 0 us
  other arithmetic: 7.26 us -> 0 us
    pallas_call x0 -> x1, Pallas kernels: none -> 68.9 us  [on_device(): pl.pallas_call(functools.partial(kernel, paths=paths, owned=owned, held=h...]
    all_to_all x3 -> x0, waiting for transfers between devices: 48.4 us -> none  [the longest x1 25 us: on_device(): lax.all_to_all(outgoing, 'path', split_axis=0, concat_axis=0, tiled=True)]
    all_to_all x3 -> x0, starting transfers between devices: 22 us -> none  [the longest x1 8.56 us: on_device(): lax.all_to_all(outgoing, 'path', split_axis=0, concat_axis=0, tiled=True)]
    reshape x4 -> x0, local copies, waits for them, and re-layouts: 9.8 us -> none  [the longest x1 4.4 us: on_device(): outgoing_back = jnp.dot(back_select, rounded, preferred_element_type=jnp....]
    dot_general x4 -> x0, matrix products: 8.22 us -> none  [the longest x1 4.98 us: on_device(): jnp.dot(weights.reshape(owned, paths * CAP).astype(jnp.bfloat16), incomin...]
    unnamed x14 -> x11, local copies, waits for them, and re-layouts: 15.1 us -> 7.24 us
    add x2 -> x0, other arithmetic: 4.66 us -> none  [the longest x1 4.66 us: on_device(): velocity = outer_momentum * past + delta]
  transfers between devices with their start and end apart: 3 -> 0, of which waited for: 3 -> 0; matrix products, arithmetic and copies ran while one was open for 12% -> 0% of each run, Pallas kernels for 0% -> 0%
where the time goes in v1:
time: 77 us; the launch traced here: 76.8 us
  Pallas kernels  68.9 us (89%)
  local copies, waits for them, and re-layouts  7.24 us (9%)
    pallas_call x1, Pallas kernels, on_device(): pl.pallas_call(functools.partial(kernel, paths=paths, owned=owned, held=h...  68.9 us
    unnamed x11, local copies, waits for them, and re-layouts  7.24 us

profile of v1, /device:TPU:1, one launch (start us, length us, event | category | flops | bytes accessed | tf_op | source)
XLA Modules:
  0.0 76.8 jit_solution(16652104198723335568)
XLA Ops:
  0.6 0.0 copy-start
  0.6 1.2 %copy-done = bf16[1,16,8,4096]{3,2,1,0:T(8,128)(2,1)S(1)} copy-done((bf16[1,16,8,4096]{3,2,1,0:T(8,128)(2,1)S(1)}, bf16[1,16,8,4096]{3,2,1,0:T(8,128)(2,1)}, u32[]{:S(2)}) %copy-start) | copy-done | bytes 1048600
  1.9 0.0 copy-start.1
  1.9 0.7 copy-done.1
  2.6 0.0 copy-start.2
  2.6 0.7 copy-done.2
  3.3 68.9 %shard_map.76 = (f32[16,256,128]{2,1,0:T(8,128)S(1)}, f32[16,256,128]{2,1,0:T(8,128)}, bf16[16,256,128]{2,1,0:T(8,128)(2,1)S(1)}) custom-call(s32[16,16]{1,0:T(8,128)S(1)} %copy-done.1, s32[16,16]{1,0:T(8,128)S(1)} %copy-done.2, bf16[16,256,128]{2,1,0:T(8,128)(2,1)S(1)} %bitcast.31, f32[16,256,128]{2,1,0:T(8,128)} %bitcast.33, f32[16,256,128]{2,1,0:T(8,128)} %bitcast.34), custom_call_target="tpu_custom_call" | custom-call | tf_op jit(solution)/shard_map/pallas_call | solution.py:321
  72.1 0.0 copy-start.3
  72.1 1.3 %copy.11 = f32[16,8,4096]{2,1,0:T(8,128)} copy(f32[16,8,4096]{2,1,0:T(8,128)S(1)} %bitcast.30) | data formatting | bytes 4194304
  73.5 1.0 %copy-done.3 = f32[16,256,128]{2,1,0:T(8,128)S(1)} copy-done((f32[16,256,128]{2,1,0:T(8,128)S(1)}, f32[16,256,128]{2,1,0:T(8,128)}, u32[]{:S(2)}) %copy-start.3) | copy-done | bytes 2097176
  74.5 1.3 %copy.12 = f32[16,8,4096]{2,1,0:T(8,128)} copy(f32[16,8,4096]{2,1,0:T(8,128)S(1)} %bitcast.35) | data formatting | bytes 4194304
  75.8 1.0 %copy.13 = bf16[1,16,8,4096]{3,2,1,0:T(8,128)(2,1)} copy(bf16[1,16,8,4096]{3,2,1,0:T(8,128)(2,1)S(1)} %bitcast.32) | data formatting | bytes 2097152
Async XLA Ops:
  0.6 1.2 %copy-start = (bf16[1,16,8,4096]{3,2,1,0:T(8,128)(2,1)S(1)}, bf16[1,16,8,4096]{3,2,1,0:T(8,128)(2,1)}, u32[]{:S(2)}) copy-start(bf16[1,16,8,4096]{3,2,1,0:T(8,128)(2,1)} %param.5) | copy-start | bytes 3145732
  1.9 0.7 copy-start.1
  2.6 0.7 copy-start.2
  72.1 2.3 %copy-start.3 = (f32[16,256,128]{2,1,0:T(8,128)S(1)}, f32[16,256,128]{2,1,0:T(8,128)}, u32[]{:S(2)}) copy-start(f32[16,256,128]{2,1,0:T(8,128)} %get-tuple-element.7) | copy-start | bytes 6291460

commit v2 on v1

v2 whole, which is shorter than its diff:
```python
import functools

import jax
import jax.numpy as jnp
from jax import lax
from jax.experimental import pallas as pl
from jax.experimental.pallas import tpu as pltpu
from jax.sharding import PartitionSpec as P

MESH = pl.DeviceIdType.MESH
CAP = 2
OUT_CHUNKS = (192, 64)
BACK_CHUNKS = (32, 224)
LANES = 128

outer_momentum = 0.9
outer_rate = 0.7
from_past = outer_rate * outer_momentum * outer_momentum
from_delta = outer_rate * (1.0 + outer_momentum)

ORDER = (
    (1, 2, 0), (1, 2, 1), (0, 2, 0), (0, 2, 1), (1, 1, 0), (1, 3, 1), (0, 1, 0), (0, 3, 1),
    (1, 1, 1), (1, 3, 0), (0, 1, 1), (0, 3, 0), (1, 0, 0), (1, 0, 1), (0, 0, 1),
)


def number(offset):
    return (offset[0] * 4 + offset[1]) * 2 + offset[2]


def path_at(me, offset, sign):
    x, y, c = me // 8, (me // 2) % 4, me % 2
    x = (x + offset[0]) % 2
    y = (y + sign * offset[1] + 4) % 4
    c = (c + offset[2]) % 2
    return (x * 4 + y) * 2 + c


def offset_of(index):
    return (index // 8, (index // 2) % 4, index % 2)


def kernel(
    ids_ref, counts_ref, params_ref, global_ref, momentum_ref, new_glob, new_mom, placed,
    *scratch, paths, owned, held, shards, rows, span,
):
    scratch = list(scratch)

    def take(n):
        taken = scratch[:n]
        del scratch[:n]
        return taken

    ids, counts, local, glob, mom, raw, parts, squares, mine, others, factor, rounded = take(12)
    pick_v, table_v, weight_v, pick, table, weight = take(6)
    out, arrived = take(len(OUT_CHUNKS)), take(len(OUT_CHUNKS))
    out_back, back = take(len(BACK_CHUNKS)), take(len(BACK_CHUNKS))
    load_sem, send_sem, recv_sem, send_back_sem, back_sem, norm_send, norm_recv = scratch
    me = lax.axis_index("path")
    shard = lax.axis_index("shard")
    starts = [sum(OUT_CHUNKS[:c]) for c in range(len(OUT_CHUNKS))]
    back_starts = [sum(BACK_CHUNKS[:c]) for c in range(len(BACK_CHUNKS))]

    load_local = pltpu.make_async_copy(params_ref, local, load_sem.at[1])
    load_ids = pltpu.make_async_copy(ids_ref, ids, load_sem.at[2])
    load_counts = pltpu.make_async_copy(counts_ref, counts, load_sem.at[3])
    load_glob = pltpu.make_async_copy(global_ref, glob, load_sem.at[4])
    load_mom = pltpu.make_async_copy(momentum_ref, mom, load_sem.at[5])
    load_ids.start()
    load_local.start()
    barrier = pltpu.get_barrier_semaphore()
    for offset in ORDER:
        pl.semaphore_signal(
            barrier, inc=1, device_id=(path_at(me, offset, 1), shard), device_id_type=MESH
        )
    zl = shards // 2
    shard_offsets = [(a, b) for a in range(2) for b in range(zl)][1:]

    def shard_at(a, b):
        return ((shard // zl + a) % 2) * zl + (shard % zl + b) % zl

    for a, b in shard_offsets:
        pl.semaphore_signal(barrier, inc=1, device_id=(me, shard_at(a, b)), device_id_type=MESH)
    for load in (load_counts, load_glob, load_mom):
        load.start()

    place = lax.broadcasted_iota(jnp.int32, (paths, held), 1)
    lane = lax.broadcasted_iota(jnp.int32, (paths, LANES), 1)
    load_ids.wait()
    my_group = lax.shift_right_logical(ids[pl.ds(me, 1), :], 4)
    goes = my_group == lax.broadcasted_iota(jnp.int32, (paths, held), 0)
    first = jnp.min(jnp.where(goes, place, held - 1), axis=1, keepdims=True)
    last = jnp.max(jnp.where(goes, place, 0), axis=1, keepdims=True)
    pick_v[...] = jnp.where(lane == 0, first, last)
    copy_pick = pltpu.make_async_copy(pick_v, pick, load_sem.at[0])
    copy_pick.start()
    copy_pick.wait()
    load_local.wait()

    def send(c, offset):
        index = number(offset)
        return pltpu.make_async_remote_copy(
            src_ref=out[c].at[index],
            dst_ref=arrived[c].at[pl.ds(index * CAP, CAP)],
            send_sem=send_sem.at[c, index],
            recv_sem=recv_sem.at[c, index],
            device_id=(path_at(me, offset, 1), shard),
            device_id_type=MESH,
        )

    for c, block in enumerate(OUT_CHUNKS):
        for index in (*map(number, ORDER), 0):
            goal = path_at(me, offset_of(index), 1)
            for r in range(CAP):
                piece = local[pick[goal, r], starts[c]:starts[c] + block, :]
                if index == 0:
                    arrived[c][r] = piece
                else:
                    out[c][index, r] = piece
        if c == 0:
            pl.semaphore_wait(barrier, len(ORDER) + len(shard_offsets))
        for offset in ORDER:
            send(c, offset).start()

    slots = CAP * paths
    load_counts.wait()
    all_ids = ids[...]
    ours = lax.shift_right_logical(all_ids, 4) == me
    local_ids = all_ids - me * owned
    tokens = counts[...].astype(jnp.float32)
    from_first = jnp.min(jnp.where(ours, place, held), axis=1, keepdims=True)
    from_last = jnp.max(jnp.where(ours, place, -1), axis=1, keepdims=True)

    def at(spot, x):
        return jnp.sum(jnp.where(ours & (place == spot), x, jnp.zeros_like(x)), axis=1, keepdims=True)

    wide = (paths, LANES)

    def both(a, b):
        return jnp.concatenate([jnp.broadcast_to(a, wide), jnp.broadcast_to(b, wide)], axis=0)

    module = both(at(from_first, local_ids), at(from_last, local_ids))
    amount = both(at(from_first, tokens), at(from_last, tokens))
    valid = both(
        jnp.where(from_last >= 0, 1, 0), jnp.where(from_last > from_first, 1, 0)
    ) > 0
    sub = lax.broadcasted_iota(jnp.int32, (slots, LANES), 0)
    col = lax.broadcasted_iota(jnp.int32, (slots, LANES), 1)

    def across(x):
        return jnp.sum(jnp.where(sub == col, x, 0), axis=0, keepdims=True)

    key = jnp.where(valid, module * slots + sub, slots * owned + sub)
    key_row = across(key)
    module_row = across(jnp.where(valid, module, owned))
    before = (key_row < key) & (col < slots)
    position = jnp.sum(jnp.where(before, 1, 0), axis=1, keepdims=True)
    again = jnp.max(jnp.where(before & (module_row == module), 1.0, 0.0), axis=1, keepdims=True)
    there = position == col
    source = sub & (paths - 1)
    sx = (lax.shift_right_logical(source, 3) + me // 8) & 1
    sy = ((me // 2) % 4 + 4 - (lax.shift_right_logical(source, 1) & 3)) & 3
    sc = ((source & 1) + me % 2) & 1
    landed = ((sx * 4 + sy) * 2 + sc) * CAP + lax.shift_right_logical(sub, 4)
    holds = valid & (module == col)
    total = jnp.sum(jnp.where(holds, amount, 0.0), axis=0, keepdims=True)
    rank = jnp.sum(jnp.where(goes & (place != first), 1, 0), axis=0, keepdims=True)
    ox = (lax.shift_right_logical(my_group, 3) + me // 8) & 1
    oy = ((me // 2) % 4 + 4 - (lax.shift_right_logical(my_group, 1) & 3)) & 3
    oc = ((my_group & 1) + me % 2) & 1
    table_v[0:1, :] = jnp.sum(jnp.where(there, landed, 0), axis=0, keepdims=True)
    table_v[1:2, :] = jnp.max(jnp.where(holds, jnp.broadcast_to(position, holds.shape), 0), axis=0, keepdims=True)
    table_v[2:3, :] = across(jnp.where(valid, module, 0))
    table_v[3:4, 0:held] = ((ox * 4 + oy) * 2 + oc) * CAP + rank
    weight_v[0:1, :] = jnp.sum(jnp.where(there & valid, amount, 0.0), axis=0, keepdims=True)
    weight_v[1:2, :] = jnp.sum(jnp.where(there, jnp.broadcast_to(again, there.shape), 0.0), axis=0, keepdims=True)
    weight_v[2:3, :] = total
    weight_v[3:4, :] = 1.0 / jnp.maximum(total, 1.0)
    weight_v[4:5, :] = jnp.where(total > 0.0, 1.0, 0.0)
    copy_table = pltpu.make_async_copy(table_v, table, load_sem.at[0])
    copy_weight = pltpu.make_async_copy(weight_v, weight, load_sem.at[1])
    copy_table.start()
    copy_weight.start()

    copy_table.wait()
    copy_weight.wait()
    load_glob.wait()
    load_mom.wait()
    for c, block in enumerate(OUT_CHUNKS):
        for offset in ORDER:
            send(c, offset).wait_recv()

        step = min(block, 64)

        for at_row in range(0, block, step):

            def running(e, acc, c=c, step=step, at_row=at_row):
                x = arrived[c][table[0, e], at_row:at_row + step, :].astype(jnp.float32)
                acc = acc * weight[1, e] + x * weight[0, e]
                parts[e, at_row:at_row + step, :] = acc
                return acc

            lax.fori_loop(0, slots, running, jnp.zeros((step, LANES), jnp.float32))

        def one_sum(m, carry, c=c, block=block):
            here = slice(starts[c], starts[c] + block)
            scale = weight[3, m]
            summed = parts[table[1, m], 0:block, :]
            part = glob[m, here, :] * (weight[2, m] * scale) - summed * (weight[4, m] * scale)
            raw[m, here, :] = part
            squared = jnp.sum((part * part).reshape(block // 8, 8, LANES), axis=0)
            if c == 0:
                squares[m] = squared
            else:
                squares[m] += squared
            return carry

        lax.fori_loop(0, owned, one_sum, 0)

    mine[...] = jnp.sum(squares[...], axis=1)
    norms = []
    for j, (a, b) in enumerate(shard_offsets):
        norm = pltpu.make_async_remote_copy(
            src_ref=mine,
            dst_ref=others.at[j],
            send_sem=norm_send.at[j],
            recv_sem=norm_recv.at[j],
            device_id=(me, shard_at(a, b)),
            device_id_type=MESH,
        )
        norm.start()
        norms.append(norm)

    def base(m, carry):
        past = mom[m]
        glob[m] = glob[m] - from_past * past
        mom[m] = outer_momentum * past
        return carry

    lax.fori_loop(0, owned, base, 0)
    for c in range(len(OUT_CHUNKS)):
        for offset in ORDER:
            send(c, offset).wait_send()
    for norm in norms:
        norm.wait()
    whole = mine[...]
    for j in range(len(shard_offsets)):
        whole = whole + others[j]
    mean = jnp.sum(whole, axis=1, keepdims=True) / span
    factor[...] = jnp.broadcast_to(
        jnp.minimum(1.0, 1.0 / jnp.sqrt(mean + 1e-06)), (owned, LANES)
    )

    def send_back(c, offset):
        index = number(offset)
        return pltpu.make_async_remote_copy(
            src_ref=out_back[c].at[index],
            dst_ref=back[c].at[pl.ds(index * CAP, CAP)],
            send_sem=send_back_sem.at[c, index],
            recv_sem=back_sem.at[c, index],
            device_id=(path_at(me, offset, 1), shard),
            device_id_type=MESH,
        )

    for c, block in enumerate(BACK_CHUNKS):

        def update(m, carry, c=c, block=block):
            here = slice(back_starts[c], back_starts[c] + block)
            delta = raw[m, here, :] * factor[pl.ds(m, 1), :]
            updated = glob[m, here, :] - from_delta * delta
            rounded[m, 0:block, :] = updated.astype(jnp.bfloat16)
            new_glob[m, here, :] = updated
            new_mom[m, here, :] = mom[m, here, :] + delta
            return carry

        lax.fori_loop(0, owned, update, 0)
        for index in (*map(number, ORDER), 0):
            goal = path_at(me, offset_of(index), 1)
            for r in range(CAP):
                piece = rounded[table[2, r * paths + goal], 0:block, :]
                if index == 0:
                    back[c][r] = piece
                else:
                    out_back[c][index, r] = piece
        for offset in ORDER:
            send_back(c, offset).start()

    for c, block in enumerate(BACK_CHUNKS):
        for offset in ORDER:
            send_back(c, offset).wait_recv()
        for k in range(held):
            placed[k, back_starts[c]:back_starts[c] + block, :] = back[c][table[3, k]]
    for c in range(len(BACK_CHUNKS)):
        for offset in ORDER:
            send_back(c, offset).wait_send()


def write_out(*refs):
    n = (len(refs) - 1) // 2
    copies = [
        pltpu.make_async_copy(source, target, refs[-1].at[i])
        for i, (source, target) in enumerate(zip(refs[:n], refs[n:2 * n]))
    ]
    for copy in copies:
        copy.start()
    for copy in copies:
        copy.wait()


def to_tiles(x):
    n, r, w = x.shape
    return x.reshape(n, r, w // LANES, LANES).transpose(0, 2, 1, 3).reshape(n, r * w // LANES, LANES)


def from_tiles(x, r):
    n, rows, _ = x.shape
    w = rows * LANES // r
    return x.reshape(n, w // LANES, r, LANES).transpose(0, 2, 1, 3).reshape(n, r, w)


def on_device(path_params, global_params, momentum, module_ids, token_counts):
    paths, held = module_ids.shape
    owned, r, width = global_params.shape
    shards = lax.axis_size("shard")
    rows = r * width // LANES
    bf, f32, i32 = jnp.bfloat16, jnp.float32, jnp.int32
    vmem, smem = pltpu.VMEM, pltpu.SMEM
    dma = pltpu.SemaphoreType.DMA
    in_hbm = pl.BlockSpec(memory_space=pltpu.HBM)
    in_vmem = pl.BlockSpec(memory_space=pltpu.VMEM)
    outs, backs = len(OUT_CHUNKS), len(BACK_CHUNKS)
    scratch = [
        vmem((paths, held), i32), vmem((paths, held), i32),
        vmem((held, rows, LANES), bf), vmem((owned, rows, LANES), f32), vmem((owned, rows, LANES), f32),
        vmem((owned, rows, LANES), f32), vmem((paths * CAP, max(OUT_CHUNKS), LANES), f32),
        vmem((owned, 8, LANES), f32), vmem((owned, LANES), f32), vmem((shards - 1, owned, LANES), f32),
        vmem((owned, LANES), f32),
        vmem((owned, max(BACK_CHUNKS), LANES), bf),
        vmem((paths, LANES), i32), vmem((8, LANES), i32), vmem((8, LANES), f32),
        smem((paths, LANES), i32), smem((8, LANES), i32), smem((8, LANES), f32),
        *[vmem((paths, CAP, block, LANES), bf) for block in OUT_CHUNKS],
        *[vmem((paths * CAP, block, LANES), bf) for block in OUT_CHUNKS],
        *[vmem((paths, CAP, block, LANES), bf) for block in BACK_CHUNKS],
        *[vmem((paths * CAP, block, LANES), bf) for block in BACK_CHUNKS],
        dma((6,)), dma((outs, paths)), dma((outs, paths)), dma((backs, paths)), dma((backs, paths)),
        dma((shards - 1,)), dma((shards - 1,)),
    ]
    shapes = (
        jax.ShapeDtypeStruct((owned, rows, LANES), f32),
        jax.ShapeDtypeStruct((owned, rows, LANES), f32),
        jax.ShapeDtypeStruct((held, rows, LANES), bf),
    )
    results = pl.pallas_call(
        functools.partial(
            kernel, paths=paths, owned=owned, held=held, shards=shards, rows=rows,
            span=r * width * shards,
        ),
        out_shape=shapes,
        in_specs=[in_hbm] * 5,
        out_specs=(in_vmem,) * 3,
        scratch_shapes=scratch,
        compiler_params=pltpu.CompilerParams(
            collective_id=0, has_side_effects=True, vmem_limit_bytes=42 * 1024 * 1024
        ),
    )(*[
        pltpu.with_memory_space_constraint(x, pltpu.HBM)
        for x in (module_ids, token_counts, to_tiles(path_params[0]), to_tiles(global_params), to_tiles(momentum))
    ])
    new_global, new_momentum, placed = pl.pallas_call(
        write_out,
        out_shape=shapes,
        in_specs=[in_vmem] * 3,
        out_specs=(in_hbm,) * 3,
        scratch_shapes=[dma((3,))],
        compiler_params=pltpu.CompilerParams(vmem_limit_bytes=8 * 1024 * 1024),
    )(*results)
    return (
        from_tiles(new_global, r),
        from_tiles(new_momentum, r),
        from_tiles(placed, r)[None],
    )


def solution(mesh):
    placed = (
        P("path", None, "shard", None),
        P("path", "shard", None),
        P("path", "shard", None),
        P(),
        P(),
    )
    return jax.shard_map(
        on_device,
        mesh=mesh,
        in_specs=placed,
        out_specs=(
            P("path", "shard", None),
            P("path", "shard", None),
            P("path", None, "shard", None),
        ),
        check_vma=False,
    )
```

time: 77 us -> 68.2 us (0.89)
  local copies, waits for them, and re-layouts: 7.24 us -> 0 us
  Pallas kernels: 68.9 us -> 67.4 us
    unnamed x11 -> x0, local copies, waits for them, and re-layouts: 7.24 us -> none
    pallas_call x1, Pallas kernels: 68.9 us -> 65.1 us  [on_device(): pl.pallas_call(functools.partial(kernel, paths=paths, owned=owned, held=h...]
    pallas_call x0 -> x1, Pallas kernels: none -> 2.38 us  [on_device(): pl.pallas_call(write_out, out_shape=shapes, in_specs=[in_vmem] * 3, out_s...]
where the time goes in v2:
time: 68.2 us; the launch traced here: 68.1 us
  Pallas kernels  67.4 us (99%)
    pallas_call x1, Pallas kernels, on_device(): pl.pallas_call(functools.partial(kernel, paths=paths, owned=owned, held=h...  65.1 us
    pallas_call x1, Pallas kernels, on_device(): pl.pallas_call(write_out, out_shape=shapes, in_specs=[in_vmem] * 3, out_s...  2.38 us

profile of v2, /device:TPU:1, one launch (start us, length us, event | category | flops | bytes accessed | tf_op | source)
XLA Modules:
  0.0 68.1 jit_solution(6973503411627623122)
XLA Ops:
  0.6 65.1 %shard_map.76 = (f32[16,256,128]{2,1,0:T(8,128)S(1)}, f32[16,256,128]{2,1,0:T(8,128)S(1)}, bf16[16,256,128]{2,1,0:T(8,128)(2,1)S(1)}) custom-call(s32[16,16]{1,0:T(8,128)} %ids_ref.1, s32[16,16]{1,0:T(8,128)} %counts_ref.1, bf16[16,256,128]{2,1,0:T(8,128)(2,1)} %bitcast.32, f32[16,256,128]{2,1,0:T(8,128)} %bitcast.30, f32[16,256,128]{2,1,0:T(8,128)} %bitcast.31), custom_call_target="tpu_custom_call" | custom-call | tf_op jit(solution)/shard_map/pallas_call | solution.py:353
  65.7 2.4 %shard_map.77 = (f32[16,256,128]{2,1,0:T(8,128)}, f32[16,256,128]{2,1,0:T(8,128)}, bf16[16,256,128]{2,1,0:T(8,128)(2,1)}) custom-call(f32[16,256,128]{2,1,0:T(8,128)S(1)} %get-tuple-element.9.refs_0_, f32[16,256,128]{2,1,0:T(8,128)S(1)} %get-tuple-element.10.refs_1_, bf16[16,256,128]{2,1,0:T(8,128)(2,1)S(1)} %get-tuple-element.11.refs_2_), custom_call_target="tpu_custom_call" | custom-call | tf_op jit(solution)/shard_map/pallas_call | solution.py:369

commit v3 on v2

--- a/solution.py
+++ b/solution.py
@@ -12,32 +12,23 @@
 OUT_CHUNKS = (192, 64)
 BACK_CHUNKS = (32, 224)
 LANES = 128
+PIECES = 1
 
 outer_momentum = 0.9
 outer_rate = 0.7
 from_past = outer_rate * outer_momentum * outer_momentum
 from_delta = outer_rate * (1.0 + outer_momentum)
 
-ORDER = (
-    (1, 2, 0), (1, 2, 1), (0, 2, 0), (0, 2, 1), (1, 1, 0), (1, 3, 1), (0, 1, 0), (0, 3, 1),
-    (1, 1, 1), (1, 3, 0), (0, 1, 1), (0, 3, 0), (1, 0, 0), (1, 0, 1), (0, 0, 1),
-)
+CHIPS = ((1, 2), (0, 2), (1, 1), (1, 3), (0, 1), (0, 3), (1, 0))
 
 
 def number(offset):
-    return (offset[0] * 4 + offset[1]) * 2 + offset[2]
-
-
-def path_at(me, offset, sign):
-    x, y, c = me // 8, (me // 2) % 4, me % 2
-    x = (x + offset[0]) % 2
-    y = (y + sign * offset[1] + 4) % 4
-    c = (c + offset[2]) % 2
-    return (x * 4 + y) * 2 + c
-
-
-def offset_of(index):
-    return (index // 8, (index // 2) % 4, index % 2)
+    return offset[0] * 4 + offset[1]
+
+
+def path_at(me, offset, core, sign=1):
+    x, y = me // 8, (me // 2) % 4
+    return ((x + offset[0]) % 2 * 4 + (y + sign * offset[1] + 4) % 4) * 2 + core
 
 
 def kernel(
@@ -58,6 +49,8 @@
     load_sem, send_sem, recv_sem, send_back_sem, back_sem, norm_send, norm_recv = scratch
     me = lax.axis_index("path")
     shard = lax.axis_index("shard")
+    core = me % 2
+    twin = me + 1 - 2 * core
     starts = [sum(OUT_CHUNKS[:c]) for c in range(len(OUT_CHUNKS))]
     back_starts = [sum(BACK_CHUNKS[:c]) for c in range(len(BACK_CHUNKS))]
 
@@ -69,10 +62,9 @@
     load_ids.start()
     load_local.start()
     barrier = pltpu.get_barrier_semaphore()
-    for offset in ORDER:
-        pl.semaphore_signal(
-            barrier, inc=1, device_id=(path_at(me, offset, 1), shard), device_id_type=MESH
-        )
+    peers = [path_at(me, offset, other) for offset in CHIPS for other in range(2)] + [twin]
+    for peer in peers:
+        pl.semaphore_signal(barrier, inc=1, device_id=(peer, shard), device_id_type=MESH)
     zl = shards // 2
     shard_offsets = [(a, b) for a in range(2) for b in range(zl)][1:]
 
@@ -97,30 +89,68 @@
     copy_pick.wait()
     load_local.wait()
 
-    def send(c, offset):
-        index = number(offset)
+    def sent(source, target, send_sems, recv_sems, c, offset, to):
+        at_home = 0 if offset is None else number(offset) * 2 + to
+        landing = core if offset is None else number(offset) * 2 + core
+        goal = twin if offset is None else path_at(me, offset, to)
         return pltpu.make_async_remote_copy(
-            src_ref=out[c].at[index],
-            dst_ref=arrived[c].at[pl.ds(index * CAP, CAP)],
-            send_sem=send_sem.at[c, index],
-            recv_sem=recv_sem.at[c, index],
-            device_id=(path_at(me, offset, 1), shard),
+            src_ref=source[c].at[at_home],
+            dst_ref=target[c].at[pl.ds(landing * CAP, CAP)],
+            send_sem=send_sems.at[c, at_home],
+            recv_sem=recv_sems.at[c, landing],
+            device_id=(goal, shard),
             device_id_type=MESH,
         )
 
+    def awaited(source, target, send_sems, recv_sems, c):
+        for offset in CHIPS:
+            for other in range(2):
+                landing = number(offset) * 2 + other
+                pltpu.make_async_remote_copy(
+                    src_ref=source[c].at[landing],
+                    dst_ref=target[c].at[pl.ds(landing * CAP, CAP)],
+                    send_sem=send_sems.at[c, landing],
+                    recv_sem=recv_sems.at[c, landing],
+                    device_id=(path_at(me, offset, other), shard),
+                    device_id_type=MESH,
+                ).wait_recv()
+        landing = 1 - core
+        pltpu.make_async_remote_copy(
+            src_ref=source[c].at[0],
+            dst_ref=target[c].at[pl.ds(landing * CAP, CAP)],
+            send_sem=send_sems.at[c, 0],
+            recv_sem=recv_sems.at[c, landing],
+            device_id=(twin, shard),
+            device_id_type=MESH,
+        ).wait_recv()
+
+    there_and = (out, arrived, send_sem, recv_sem)
+    and_back = (out_back, back, send_back_sem, back_sem)
+
+    def send_half(blocks, to):
+        for c in range(len(OUT_CHUNKS)):
+            for offset, _ in blocks:
+                sent(*there_and, c, offset, to).start()
+
+    for to in range(2):
+        blocks = [(offset, to) for offset in CHIPS]
+        if to == 0:
+            blocks = [(None, None)] + blocks
+        for c, block in enumerate(OUT_CHUNKS):
+            here = slice(starts[c], starts[c] + block)
+            for offset, _ in blocks:
+                goal = twin if offset is None else path_at(me, offset, to)
+                at_home = 0 if offset is None else number(offset) * 2 + to
+                for r in range(CAP):
+                    out[c][at_home, r] = local[pick[goal, r], here, :]
+        if to == 0:
+            pl.semaphore_wait(barrier, len(peers) + len(shard_offsets))
+            send_half(blocks, to)
+        else:
+            pl.when(core == 1)(functools.partial(send_half, blocks, to))
     for c, block in enumerate(OUT_CHUNKS):
-        for index in (*map(number, ORDER), 0):
-            goal = path_at(me, offset_of(index), 1)
-            for r in range(CAP):
-                piece = local[pick[goal, r], starts[c]:starts[c] + block, :]
-                if index == 0:
-                    arrived[c][r] = piece
-                else:
-                    out[c][index, r] = piece
-        if c == 0:
-            pl.semaphore_wait(barrier, len(ORDER) + len(shard_offsets))
-        for offset in ORDER:
-            send(c, offset).start()
+        for r in range(CAP):
+            arrived[c][core * CAP + r] = local[pick[me, r], starts[c]:starts[c] + block, :]
 
     slots = CAP * paths
     load_counts.wait()
@@ -160,14 +190,14 @@
     source = sub & (paths - 1)
     sx = (lax.shift_right_logical(source, 3) + me // 8) & 1
     sy = ((me // 2) % 4 + 4 - (lax.shift_right_logical(source, 1) & 3)) & 3
-    sc = ((source & 1) + me % 2) & 1
+    sc = source & 1
     landed = ((sx * 4 + sy) * 2 + sc) * CAP + lax.shift_right_logical(sub, 4)
     holds = valid & (module == col)
     total = jnp.sum(jnp.where(holds, amount, 0.0), axis=0, keepdims=True)
     rank = jnp.sum(jnp.where(goes & (place != first), 1, 0), axis=0, keepdims=True)
     ox = (lax.shift_right_logical(my_group, 3) + me // 8) & 1
     oy = ((me // 2) % 4 + 4 - (lax.shift_right_logical(my_group, 1) & 3)) & 3
-    oc = ((my_group & 1) + me % 2) & 1
+    oc = my_group & 1
     table_v[0:1, :] = jnp.sum(jnp.where(there, landed, 0), axis=0, keepdims=True)
     table_v[1:2, :] = jnp.max(jnp.where(holds, jnp.broadcast_to(position, holds.shape), 0), axis=0, keepdims=True)
     table_v[2:3, :] = across(jnp.where(valid, module, 0))
@@ -187,8 +217,7 @@
     load_glob.wait()
     load_mom.wait()
     for c, block in enumerate(OUT_CHUNKS):
-        for offset in ORDER:
-            send(c, offset).wait_recv()
+        awaited(*there_and, c)
 
         step = min(block, 64)
 
@@ -230,6 +259,7 @@
         )
         norm.start()
         norms.append(norm)
+    pl.when(core == 0)(functools.partial(send_half, blocks, 1))
 
     def base(m, carry):
         past = mom[m]
@@ -238,9 +268,6 @@
         return carry
 
     lax.fori_loop(0, owned, base, 0)
-    for c in range(len(OUT_CHUNKS)):
-        for offset in ORDER:
-            send(c, offset).wait_send()
     for norm in norms:
         norm.wait()
     whole = mine[...]
@@ -251,17 +278,7 @@
         jnp.minimum(1.0, 1.0 / jnp.sqrt(mean + 1e-06)), (owned, LANES)
     )
 
-    def send_back(c, offset):
-        index = number(offset)
-        return pltpu.make_async_remote_copy(
-            src_ref=out_back[c].at[index],
-            dst_ref=back[c].at[pl.ds(index * CAP, CAP)],
-            send_sem=send_back_sem.at[c, index],
-            recv_sem=back_sem.at[c, index],
-            device_id=(path_at(me, offset, 1), shard),
-            device_id_type=MESH,
-        )
-
+    targets = [(offset, to) for offset in CHIPS for to in range(2)] + [(None, None)]
     for c, block in enumerate(BACK_CHUNKS):
 
         def update(m, carry, c=c, block=block):
@@ -274,33 +291,34 @@
             return carry
 
         lax.fori_loop(0, owned, update, 0)
-        for index in (*map(number, ORDER), 0):
-            goal = path_at(me, offset_of(index), 1)
+        for offset, to in targets:
+            goal = twin if offset is None else path_at(me, offset, to)
+            at_home = 0 if offset is None else number(offset) * 2 + to
             for r in range(CAP):
-                piece = rounded[table[2, r * paths + goal], 0:block, :]
-                if index == 0:
-                    back[c][r] = piece
-                else:
-                    out_back[c][index, r] = piece
-        for offset in ORDER:
-            send_back(c, offset).start()
+                out_back[c][at_home, r] = rounded[table[2, r * paths + goal], 0:block, :]
+        for offset, to in targets:
+            sent(*and_back, c, offset, to).start()
+        for r in range(CAP):
+            back[c][core * CAP + r] = rounded[table[2, r * paths + me], 0:block, :]
 
     for c, block in enumerate(BACK_CHUNKS):
-        for offset in ORDER:
-            send_back(c, offset).wait_recv()
+        awaited(*and_back, c)
         for k in range(held):
             placed[k, back_starts[c]:back_starts[c] + block, :] = back[c][table[3, k]]
-    for c in range(len(BACK_CHUNKS)):
-        for offset in ORDER:
-            send_back(c, offset).wait_send()
+    for way, chunks in ((there_and, OUT_CHUNKS), (and_back, BACK_CHUNKS)):
+        for c in range(len(chunks)):
+            for offset, to in targets:
+                sent(*way, c, offset, to).wait_send()
 
 
 def write_out(*refs):
     n = (len(refs) - 1) // 2
-    copies = [
-        pltpu.make_async_copy(source, target, refs[-1].at[i])
-        for i, (source, target) in enumerate(zip(refs[:n], refs[n:2 * n]))
-    ]
+    copies = []
+    for i, (source, target) in enumerate(zip(refs[:n], refs[n:2 * n])):
+        piece = source.shape[0] // PIECES
+        for j in range(PIECES):
+            here = pl.ds(j * piece, piece)
+            copies.append(pltpu.make_async_copy(source.at[here], target.at[here], refs[-1].at[i, j]))
     for copy in copies:
         copy.start()
     for copy in copies:
@@ -371,7 +389,7 @@
         out_shape=shapes,
         in_specs=[in_vmem] * 3,
         out_specs=(in_hbm,) * 3,
-        scratch_shapes=[dma((3,))],
+        scratch_shapes=[dma((3, PIECES))],
         compiler_params=pltpu.CompilerParams(vmem_limit_bytes=8 * 1024 * 1024),
     )(*results)
     return (

time: 68.2 us -> 62.6 us (0.918)
  Pallas kernels: 67.4 us -> 61.9 us
    pallas_call x1, Pallas kernels: 65.1 us -> 59.5 us  [on_device(): pl.pallas_call(functools.partial(kernel, paths=paths, owned=owned, held=h...]
where the time goes in v3:
time: 62.6 us; the launch traced here: 62.5 us
  Pallas kernels  61.9 us (99%)
  between operations  0.64 us (1%)
    pallas_call x1, Pallas kernels, on_device(): pl.pallas_call(functools.partial(kernel, paths=paths, owned=owned, held=h...  59.5 us
    pallas_call x1, Pallas kernels, on_device(): pl.pallas_call(write_out, out_shape=shapes, in_specs=[in_vmem] * 3, out_s...  2.38 us

profile of v3, /device:TPU:1, one launch (start us, length us, event | category | flops | bytes accessed | tf_op | source)
XLA Modules:
  0.0 62.5 jit_solution(6151713469270801960)
XLA Ops:
  0.6 59.5 %shard_map.76 = (f32[16,256,128]{2,1,0:T(8,128)S(1)}, f32[16,256,128]{2,1,0:T(8,128)S(1)}, bf16[16,256,128]{2,1,0:T(8,128)(2,1)S(1)}) custom-call(s32[16,16]{1,0:T(8,128)} %ids_ref.1, s32[16,16]{1,0:T(8,128)} %counts_ref.1, bf16[16,256,128]{2,1,0:T(8,128)(2,1)} %bitcast.32, f32[16,256,128]{2,1,0:T(8,128)} %bitcast.30, f32[16,256,128]{2,1,0:T(8,128)} %bitcast.31), custom_call_target="tpu_custom_call" | custom-call | tf_op jit(solution)/shard_map/pallas_call | solution.py:371
  60.1 2.4 %shard_map.77 = (f32[16,256,128]{2,1,0:T(8,128)}, f32[16,256,128]{2,1,0:T(8,128)}, bf16[16,256,128]{2,1,0:T(8,128)(2,1)}) custom-call(f32[16,256,128]{2,1,0:T(8,128)S(1)} %get-tuple-element.9.refs_0_, f32[16,256,128]{2,1,0:T(8,128)S(1)} %get-tuple-element.10.refs_1_, bf16[16,256,128]{2,1,0:T(8,128)(2,1)S(1)} %get-tuple-element.11.refs_2_), custom_call_target="tpu_custom_call" | custom-call | tf_op jit(solution)/shard_map/pallas_call | solution.py:387

commit v4 on v3

--- a/solution.py
+++ b/solution.py
@@ -19,7 +19,9 @@
 from_past = outer_rate * outer_momentum * outer_momentum
 from_delta = outer_rate * (1.0 + outer_momentum)
 
-CHIPS = ((1, 2), (0, 2), (1, 1), (1, 3), (0, 1), (0, 3), (1, 0))
+NEAR = ((0, 2), (1, 0), (0, 1), (0, 3))
+FAR = ((1, 2), (1, 1), (1, 3))
+CHIPS = FAR + NEAR
 
 
 def number(offset):
@@ -46,7 +48,7 @@
     pick_v, table_v, weight_v, pick, table, weight = take(6)
     out, arrived = take(len(OUT_CHUNKS)), take(len(OUT_CHUNKS))
     out_back, back = take(len(BACK_CHUNKS)), take(len(BACK_CHUNKS))
-    load_sem, send_sem, recv_sem, send_back_sem, back_sem, norm_send, norm_recv = scratch
+    load_sem, send_sem, recv_sem, send_back_sem, back_sem, norm_send, norm_recv, across_x, across_z = scratch
     me = lax.axis_index("path")
     shard = lax.axis_index("shard")
     core = me % 2
@@ -62,8 +64,8 @@
     load_ids.start()
     load_local.start()
     barrier = pltpu.get_barrier_semaphore()
-    peers = [path_at(me, offset, other) for offset in CHIPS for other in range(2)] + [twin]
-    for peer in peers:
+    near = [path_at(me, offset, other) for offset in NEAR for other in range(2)] + [twin]
+    for peer in near:
         pl.semaphore_signal(barrier, inc=1, device_id=(peer, shard), device_id_type=MESH)
     zl = shards // 2
     shard_offsets = [(a, b) for a in range(2) for b in range(zl)][1:]
@@ -71,7 +73,8 @@
     def shard_at(a, b):
         return ((shard // zl + a) % 2) * zl + (shard % zl + b) % zl
 
-    for a, b in shard_offsets:
+    near_shards = [offset for offset in shard_offsets if offset != (1, zl // 2)]
+    for a, b in near_shards:
         pl.semaphore_signal(barrier, inc=1, device_id=(me, shard_at(a, b)), device_id_type=MESH)
     for load in (load_counts, load_glob, load_mom):
         load.start()
@@ -129,25 +132,34 @@
 
     def send_half(blocks, to):
         for c in range(len(OUT_CHUNKS)):
-            for offset, _ in blocks:
+            for offset in blocks:
                 sent(*there_and, c, offset, to).start()
 
     for to in range(2):
-        blocks = [(offset, to) for offset in CHIPS]
+        blocks = [*NEAR, *FAR]
         if to == 0:
-            blocks = [(None, None)] + blocks
+            blocks = [None] + blocks
         for c, block in enumerate(OUT_CHUNKS):
             here = slice(starts[c], starts[c] + block)
-            for offset, _ in blocks:
+            for offset in blocks:
                 goal = twin if offset is None else path_at(me, offset, to)
                 at_home = 0 if offset is None else number(offset) * 2 + to
                 for r in range(CAP):
                     out[c][at_home, r] = local[pick[goal, r], here, :]
         if to == 0:
-            pl.semaphore_wait(barrier, len(peers) + len(shard_offsets))
-            send_half(blocks, to)
+            pl.semaphore_wait(barrier, len(near) + len(near_shards))
+            for dy in range(1, 4):
+                pl.semaphore_signal(
+                    across_x, inc=1, device_id=(path_at(me, (0, dy), core), shard), device_id_type=MESH
+                )
+            pl.semaphore_signal(
+                across_z, inc=1, device_id=(me, shard_at(1, 0)), device_id_type=MESH
+            )
+            send_half((None, *NEAR), 0)
+            pl.semaphore_wait(across_x, 3)
+            send_half(FAR, 0)
         else:
-            pl.when(core == 1)(functools.partial(send_half, blocks, to))
+            pl.when(core == 1)(functools.partial(send_half, blocks, 1))
     for c, block in enumerate(OUT_CHUNKS):
         for r in range(CAP):
             arrived[c][core * CAP + r] = local[pick[me, r], starts[c]:starts[c] + block, :]
@@ -247,6 +259,7 @@
         lax.fori_loop(0, owned, one_sum, 0)
 
     mine[...] = jnp.sum(squares[...], axis=1)
+    pl.semaphore_wait(across_z, 1)
     norms = []
     for j, (a, b) in enumerate(shard_offsets):
         norm = pltpu.make_async_remote_copy(
@@ -362,6 +375,7 @@
         *[vmem((paths * CAP, block, LANES), bf) for block in BACK_CHUNKS],
         dma((6,)), dma((outs, paths)), dma((outs, paths)), dma((backs, paths)), dma((backs, paths)),
         dma((shards - 1,)), dma((shards - 1,)),
+        pltpu.SemaphoreType.REGULAR, pltpu.SemaphoreType.REGULAR,
     ]
     shapes = (
         jax.ShapeDtypeStruct((owned, rows, LANES), f32),

time: 62.6 us -> 60.5 us (0.966)
  Pallas kernels: 61.9 us -> 59.7 us
    pallas_call x1, Pallas kernels: 59.5 us -> 57.3 us  [on_device(): pl.pallas_call(functools.partial(kernel, paths=paths, owned=owned, held=h...]
where the time goes in v4:
time: 60.5 us; the launch traced here: 60.4 us
  Pallas kernels  59.7 us (99%)
  between operations  0.64 us (1%)
    pallas_call x1, Pallas kernels, on_device(): pl.pallas_call(functools.partial(kernel, paths=paths, owned=owned, held=h...  57.3 us
    pallas_call x1, Pallas kernels, on_device(): pl.pallas_call(write_out, out_shape=shapes, in_specs=[in_vmem] * 3, out_s...  2.38 us

profile of v4, /device:TPU:1, one launch (start us, length us, event | category | flops | bytes accessed | tf_op | source)
XLA Modules:
  0.0 60.4 jit_solution(4574571771542482009)
XLA Ops:
  0.6 57.3 %shard_map.76 = (f32[16,256,128]{2,1,0:T(8,128)S(1)}, f32[16,256,128]{2,1,0:T(8,128)S(1)}, bf16[16,256,128]{2,1,0:T(8,128)(2,1)S(1)}) custom-call(s32[16,16]{1,0:T(8,128)} %ids_ref.1, s32[16,16]{1,0:T(8,128)} %counts_ref.1, bf16[16,256,128]{2,1,0:T(8,128)(2,1)} %bitcast.32, f32[16,256,128]{2,1,0:T(8,128)} %bitcast.30, f32[16,256,128]{2,1,0:T(8,128)} %bitcast.31), custom_call_target="tpu_custom_call" | custom-call | tf_op jit(solution)/shard_map/pallas_call | solution.py:385
  58.0 2.4 %shard_map.77 = (f32[16,256,128]{2,1,0:T(8,128)}, f32[16,256,128]{2,1,0:T(8,128)}, bf16[16,256,128]{2,1,0:T(8,128)(2,1)}) custom-call(f32[16,256,128]{2,1,0:T(8,128)S(1)} %get-tuple-element.9.refs_0_, f32[16,256,128]{2,1,0:T(8,128)S(1)} %get-tuple-element.10.refs_1_, bf16[16,256,128]{2,1,0:T(8,128)(2,1)S(1)} %get-tuple-element.11.refs_2_), custom_call_target="tpu_custom_call" | custom-call | tf_op jit(solution)/shard_map/pallas_call | solution.py:401

commit v5 on v4

--- a/solution.py
+++ b/solution.py
@@ -10,7 +10,7 @@
 MESH = pl.DeviceIdType.MESH
 CAP = 2
 OUT_CHUNKS = (192, 64)
-BACK_CHUNKS = (32, 224)
+BACK_CHUNKS = (256,)
 LANES = 128
 PIECES = 1
 
@@ -241,15 +241,17 @@
                 parts[e, at_row:at_row + step, :] = acc
                 return acc
 
-            lax.fori_loop(0, slots, running, jnp.zeros((step, LANES), jnp.float32))
-
-        def one_sum(m, carry, c=c, block=block):
-            here = slice(starts[c], starts[c] + block)
+            lax.fori_loop(0, slots, running, jnp.zeros((step, LANES), jnp.float32), unroll=8)
+
+        def one_sum(m, carry, c=c, block=block, step=step):
             scale = weight[3, m]
-            summed = parts[table[1, m], 0:block, :]
-            part = glob[m, here, :] * (weight[2, m] * scale) - summed * (weight[4, m] * scale)
-            raw[m, here, :] = part
-            squared = jnp.sum((part * part).reshape(block // 8, 8, LANES), axis=0)
+            have, want, at = weight[2, m] * scale, weight[4, m] * scale, table[1, m]
+            squared = jnp.zeros((8, LANES), jnp.float32)
+            for at_row in range(0, block, step):
+                here = slice(starts[c] + at_row, starts[c] + at_row + step)
+                part = glob[m, here, :] * have - parts[at, at_row:at_row + step, :] * want
+                raw[m, here, :] = part
+                squared = squared + jnp.sum((part * part).reshape(step // 8, 8, LANES), axis=0)
             if c == 0:
                 squares[m] = squared
             else:

time: 60.5 us -> 60.1 us (level)
  no operation moved by 1% of the time
where the time goes in v5:
time: 60.1 us; the launch traced here: 60 us
  Pallas kernels  59.3 us (99%)
  between operations  0.64 us (1%)
    pallas_call x1, Pallas kernels, on_device(): pl.pallas_call(functools.partial(kernel, paths=paths, owned=owned, held=h...  57 us
    pallas_call x1, Pallas kernels, on_device(): pl.pallas_call(write_out, out_shape=shapes, in_specs=[in_vmem] * 3, out_s...  2.38 us

profile of v5, /device:TPU:1, one launch (start us, length us, event | category | flops | bytes accessed | tf_op | source)
XLA Modules:
  0.0 60.0 jit_solution(9947643323608854514)
XLA Ops:
  0.6 57.0 %shard_map.76 = (f32[16,256,128]{2,1,0:T(8,128)S(1)}, f32[16,256,128]{2,1,0:T(8,128)S(1)}, bf16[16,256,128]{2,1,0:T(8,128)(2,1)S(1)}) custom-call(s32[16,16]{1,0:T(8,128)} %ids_ref.1, s32[16,16]{1,0:T(8,128)} %counts_ref.1, bf16[16,256,128]{2,1,0:T(8,128)(2,1)} %bitcast.32, f32[16,256,128]{2,1,0:T(8,128)} %bitcast.30, f32[16,256,128]{2,1,0:T(8,128)} %bitcast.31), custom_call_target="tpu_custom_call" | custom-call | tf_op jit(solution)/shard_map/pallas_call | solution.py:387
  57.6 2.4 %shard_map.77 = (f32[16,256,128]{2,1,0:T(8,128)}, f32[16,256,128]{2,1,0:T(8,128)}, bf16[16,256,128]{2,1,0:T(8,128)(2,1)}) custom-call(f32[16,256,128]{2,1,0:T(8,128)S(1)} %get-tuple-element.9.refs_0_, f32[16,256,128]{2,1,0:T(8,128)S(1)} %get-tuple-element.10.refs_1_, bf16[16,256,128]{2,1,0:T(8,128)(2,1)S(1)} %get-tuple-element.11.refs_2_), custom_call_target="tpu_custom_call" | custom-call | tf_op jit(solution)/shard_map/pallas_call | solution.py:403

commit v6 on v5

--- a/solution.py
+++ b/solution.py
@@ -130,15 +130,7 @@
     there_and = (out, arrived, send_sem, recv_sem)
     and_back = (out_back, back, send_back_sem, back_sem)
 
-    def send_half(blocks, to):
-        for c in range(len(OUT_CHUNKS)):
-            for offset in blocks:
-                sent(*there_and, c, offset, to).start()
-
-    for to in range(2):
-        blocks = [*NEAR, *FAR]
-        if to == 0:
-            blocks = [None] + blocks
+    def fill(blocks, to):
         for c, block in enumerate(OUT_CHUNKS):
             here = slice(starts[c], starts[c] + block)
             for offset in blocks:
@@ -146,6 +138,15 @@
                 at_home = 0 if offset is None else number(offset) * 2 + to
                 for r in range(CAP):
                     out[c][at_home, r] = local[pick[goal, r], here, :]
+
+    def send_half(blocks, to):
+        for c in range(len(OUT_CHUNKS)):
+            for offset in blocks:
+                sent(*there_and, c, offset, to).start()
+
+    for to in range(2):
+        blocks = [*NEAR, *FAR]
+        fill((None, *NEAR) if to == 0 else blocks, to)
         if to == 0:
             pl.semaphore_wait(barrier, len(near) + len(near_shards))
             for dy in range(1, 4):
@@ -156,6 +157,7 @@
                 across_z, inc=1, device_id=(me, shard_at(1, 0)), device_id_type=MESH
             )
             send_half((None, *NEAR), 0)
+            fill(FAR, 0)
             pl.semaphore_wait(across_x, 3)
             send_half(FAR, 0)
         else:

time: 60.1 us -> 60.1 us (level)
  no operation moved by 1% of the time
where the time goes in v6:
time: 60.1 us; the launch traced here: 60 us
  Pallas kernels  59.3 us (99%)
  between operations  0.64 us (1%)
    pallas_call x1, Pallas kernels, on_device(): pl.pallas_call(functools.partial(kernel, paths=paths, owned=owned, held=h...  57 us
    pallas_call x1, Pallas kernels, on_device(): pl.pallas_call(write_out, out_shape=shapes, in_specs=[in_vmem] * 3, out_s...  2.38 us

profile of v6, /device:TPU:1, one launch (start us, length us, event | category | flops | bytes accessed | tf_op | source)
XLA Modules:
  0.0 60.0 jit_solution(17879280706261454851)
XLA Ops:
  0.6 57.0 %shard_map.76 = (f32[16,256,128]{2,1,0:T(8,128)S(1)}, f32[16,256,128]{2,1,0:T(8,128)S(1)}, bf16[16,256,128]{2,1,0:T(8,128)(2,1)S(1)}) custom-call(s32[16,16]{1,0:T(8,128)} %ids_ref.1, s32[16,16]{1,0:T(8,128)} %counts_ref.1, bf16[16,256,128]{2,1,0:T(8,128)(2,1)} %bitcast.32, f32[16,256,128]{2,1,0:T(8,128)} %bitcast.30, f32[16,256,128]{2,1,0:T(8,128)} %bitcast.31), custom_call_target="tpu_custom_call" | custom-call | tf_op jit(solution)/shard_map/pallas_call | solution.py:389
  57.6 2.4 %shard_map.77 = (f32[16,256,128]{2,1,0:T(8,128)}, f32[16,256,128]{2,1,0:T(8,128)}, bf16[16,256,128]{2,1,0:T(8,128)(2,1)}) custom-call(f32[16,256,128]{2,1,0:T(8,128)S(1)} %get-tuple-element.9.refs_0_, f32[16,256,128]{2,1,0:T(8,128)S(1)} %get-tuple-element.10.refs_1_, bf16[16,256,128]{2,1,0:T(8,128)(2,1)S(1)} %get-tuple-element.11.refs_2_), custom_call_target="tpu_custom_call" | custom-call | tf_op jit(solution)/shard_map/pallas_call | solution.py:405
